TPU v7x, 32 devices: a whole 2x2x4 slice. The times are simulated.
32 devices in a mesh: groups: 2 (over x), seq: 16 (over z, y, core), sub: 1.
Axes of the slice: x: 2, y: 2, z: 4, core: 2. Of those that a mesh axis runs over, the one named last changes fastest.
Arguments:
- hidden_input: bfloat16 [16384, 4096], P(('groups', 'seq')), parts along dimension 0, may hold values from -4 to 4
- norm_gain_vector: bfloat16 [4096], replicated, may hold values from 0.099609375 to 1.8984375
- query_weight: bfloat16 [4096, 2048], P('seq', 'sub'), may hold values from -0.109375 to 0.109375
- key_value_weight: bfloat16 [4096, 2, 512], P('seq', None, 'sub'), may hold values from -0.109375 to 0.109375
- output_weight: bfloat16 [2048, 4096], P('sub', 'seq'), may hold values from -0.125 to 0.125
- adapter_input_down: bfloat16 [32, 4096, 192], P('seq'), may hold values from -0.09375 to 0.09375
- adapter_query_up: bfloat16 [32, 64, 2048], P('seq', None, 'sub'), may hold values from -0.75 to 0.75
- adapter_key_value_up: bfloat16 [32, 2, 64, 512], P('seq', None, None, 'sub'), may hold values from -0.75 to 0.75
- adapter_output_down: bfloat16 [32, 2048, 64], P('seq', 'sub'), may hold values from -0.125 to 0.125
- adapter_output_up: bfloat16 [32, 64, 4096], P('seq', None, 'sub'), may hold values from -0.75 to 0.75
- request_lengths: int32 [8], P('groups'), parts along dimension 0, may hold values from 1 to 4608, 8192 in all
- request_adapter: int32 [8], P('groups'), parts along dimension 0, may hold values from 0 to 31
- adapter_table_slot: int32 [32], replicated, may hold values from 0 to 31, each once
Outputs:
- block_out: bfloat16 [16384, 4096], P(('groups', 'seq'), 'sub'), parts along dimension 0
There are 2 independent parts, one for each index of `groups`. A program takes and returns all parts, laid end to end along the dimension named above; an argument that names none is the same for every part. Nothing has to cross between parts.
Inputs may be any that keep to these rules, and one draw needn't show every extreme that they name: `request_lengths`: the lengths add up to 8192; the longest request has exactly 4608 tokens. `request_adapter`: several requests may name the same adapter. `adapter_table_slot`: each slot holds one adapter.
All inputs are finite; a program needn't handle non-finite values.
Results may differ from a plain program's by a relative error of at most 0.013.
The roundings to bfloat16 on the way count: a program that leaves them out, or rounds other values in their place, can miss the bound.
Values may be sent and summed in bfloat16 or wider, within the bound.
No kernel may reach another device: no remote copies, remote signals or barrier semaphores. Data moves between devices by JAX's collectives and lax.ppermute only.
A program may use at most 448 MiB of HBM per device.

v0:
```python
import jax
import jax.numpy as jnp
from jax import lax
from jax.sharding import PartitionSpec as P

HEAD_WIDTH = 128
WINDOW = 4096
epsilon = 1e-05
adapter_scale = 2.0
rope_base = 10000.0
neg_big = -1e30


def spread(shard, axis, root):
    mine = lax.axis_index(axis) == root
    return lax.psum(jnp.where(mine, shard, jnp.zeros_like(shard)), axis)


def doc_index(positions, doc_ends):
    return jnp.sum((doc_ends[None, :] <= positions[:, None]).astype(jnp.int32), axis=1)


def rotary_apply(heads, request_offsets):
    half_size = heads.shape[-1] // 2
    frequency = rope_base ** (-jnp.arange(half_size, dtype=jnp.float32) * (2.0 / heads.shape[-1]))
    angles = request_offsets.astype(jnp.float32)[:, None] * frequency[None, :]
    cosine = jnp.cos(angles)[:, None, :]
    sine = jnp.sin(angles)[:, None, :]
    first_half = heads[..., :half_size]
    second_half = heads[..., half_size:]
    return jnp.concatenate(
        [first_half * cosine - second_half * sine, second_half * cosine + first_half * sine],
        axis=-1,
    )


def allowed_pairs(query_pos, query_doc, key_pos, doc_ends):
    key_doc = doc_index(key_pos, doc_ends)
    distance = query_pos[:, None] - key_pos[None, :]
    return (
        (query_doc[:, None] == key_doc[None, :])
        & (distance >= 0)
        & (distance < WINDOW)
        & (key_pos[None, :] >= 0)
    )


def shards(
    hidden_input,
    norm_gain_vector,
    query_weight,
    key_value_weight,
    output_weight,
    adapter_input_down,
    adapter_query_up,
    adapter_key_value_up,
    adapter_output_down,
    adapter_output_up,
    request_lengths,
    request_adapter,
    adapter_table_slot,
):
    row_total = hidden_input.shape[0]
    seq_index = lax.axis_index("seq")
    positions = seq_index * row_total + jnp.arange(row_total, dtype=jnp.int32)
    doc_ends = jnp.cumsum(request_lengths)
    doc_ids = doc_index(positions, doc_ends)
    request_count = request_lengths.shape[0]
    member_mask = doc_ids[:, None] == jnp.arange(request_count, dtype=jnp.int32)[None, :]
    begins = doc_ends - request_lengths
    request_offsets = positions - jnp.sum(jnp.where(member_mask, begins[None, :], 0), axis=1)
    widened = hidden_input.astype(jnp.float32)
    normed_hidden = (
        widened
        * lax.rsqrt(jnp.mean(widened * widened, axis=-1, keepdims=True) + epsilon)
        * norm_gain_vector.astype(jnp.float32)
    ).astype(jnp.bfloat16)
    query_cols = query_weight.shape[1]
    kv_cols = key_value_weight.shape[2]
    piece_query = lax.all_gather(query_weight, "seq", axis=0, tiled=True)
    piece_kv = lax.all_gather(key_value_weight, "seq", axis=0, tiled=True)
    query_base_rows = jnp.dot(normed_hidden, piece_query, preferred_element_type=jnp.float32)
    key_value_base = jnp.einsum(
        "td,dck->tck", normed_hidden, piece_kv, preferred_element_type=jnp.float32
    )
    local_total = adapter_input_down.shape[0]
    adapter_rank_size = adapter_input_down.shape[2] // 3
    query_adapter_delta = jnp.zeros((row_total, query_cols), jnp.float32)
    key_adapter_delta = jnp.zeros((row_total, kv_cols), jnp.float32)
    value_adapter_delta = jnp.zeros((row_total, kv_cols), jnp.float32)
    out_adapters = []
    for request_number in range(request_count):
        table_slot = adapter_table_slot[request_adapter[request_number]]
        owner_request = table_slot // local_total
        local_position = table_slot % local_total
        down_weight, up_query, up_kv, out_in, out_up = (
            spread(adapter_input_down[local_position], "seq", owner_request),
            spread(adapter_query_up[local_position], "seq", owner_request),
            spread(adapter_key_value_up[local_position], "seq", owner_request),
            spread(adapter_output_down[local_position], "seq", owner_request),
            spread(adapter_output_up[local_position], "seq", owner_request),
        )
        chosen = member_mask[:, request_number : request_number + 1]
        down_rows = jnp.where(
            chosen, jnp.dot(normed_hidden, down_weight, preferred_element_type=jnp.float32), 0.0
        ).astype(jnp.bfloat16)
        query_adapter_delta = query_adapter_delta + jnp.dot(
            down_rows[:, :adapter_rank_size], up_query, preferred_element_type=jnp.float32
        )
        key_adapter_delta = key_adapter_delta + jnp.dot(
            down_rows[:, adapter_rank_size : 2 * adapter_rank_size],
            up_kv[0],
            preferred_element_type=jnp.float32,
        )
        value_adapter_delta = value_adapter_delta + jnp.dot(
            down_rows[:, 2 * adapter_rank_size :], up_kv[1], preferred_element_type=jnp.float32
        )
        out_adapters.append((out_in, out_up))
    query_head_list = query_cols // HEAD_WIDTH
    key_value_heads = kv_cols // HEAD_WIDTH
    group_width = query_head_list // key_value_heads
    queries = rotary_apply(
        (query_base_rows + adapter_scale * query_adapter_delta).reshape(
            row_total, query_head_list, HEAD_WIDTH
        ),
        request_offsets,
    ).astype(jnp.bfloat16)
    queries = queries.reshape(row_total, key_value_heads, group_width, HEAD_WIDTH)
    key_row_list = rotary_apply(
        (key_value_base[:, 0] + adapter_scale * key_adapter_delta).reshape(
            row_total, key_value_heads, HEAD_WIDTH
        ),
        request_offsets,
    ).astype(jnp.bfloat16)
    value_row_list = (key_value_base[:, 1] + adapter_scale * value_adapter_delta).astype(
        jnp.bfloat16
    )
    kv_rows = jnp.stack([key_row_list.reshape(row_total, kv_cols), value_row_list], axis=1)
    piece = lax.all_gather(kv_rows, "seq", axis=0, tiled=True)
    running_max = jnp.full((key_value_heads, group_width, row_total), neg_big, jnp.float32)
    piece_len = piece.shape[0]
    key_pos = jnp.arange(piece_len, dtype=jnp.int32)
    key_heads = piece[:, 0].reshape(piece_len, key_value_heads, HEAD_WIDTH)
    value_heads = piece[:, 1].reshape(piece_len, key_value_heads, HEAD_WIDTH)
    score_matrix = jnp.einsum(
        "xouc,boc->ouxb", queries, key_heads, preferred_element_type=jnp.float32
    ) * HEAD_WIDTH ** (-0.5)
    allowed = allowed_pairs(positions, doc_ids, key_pos, doc_ends)
    score_matrix = jnp.where(allowed, score_matrix, neg_big)
    new_max = jnp.maximum(running_max, jnp.max(score_matrix, axis=-1))
    weights = jnp.where(allowed, jnp.exp(score_matrix - new_max[..., None]), 0.0)
    running_sum = jnp.sum(weights, axis=-1)
    weighted = jnp.einsum(
        "kgts,skd->kgtd",
        weights.astype(jnp.bfloat16),
        value_heads,
        preferred_element_type=jnp.float32,
    )
    mixed = weighted / running_sum[..., None]
    attended_rows = (
        jnp.transpose(mixed, (2, 0, 1, 3)).reshape(row_total, query_cols).astype(jnp.bfloat16)
    )
    out_sum = jnp.zeros((row_total, adapter_rank_size), jnp.float32)
    for request_number in range(request_count):
        output_product = jnp.dot(
            attended_rows, out_adapters[request_number][0], preferred_element_type=jnp.float32
        )
        out_sum = out_sum + jnp.where(
            member_mask[:, request_number : request_number + 1], output_product, 0.0
        )
    out_down = lax.psum(out_sum.astype(jnp.bfloat16), "sub")
    output_adapter_delta = jnp.zeros((row_total, adapter_output_up.shape[2]), jnp.float32)
    for request_number in range(request_count):
        input_rows = jnp.where(
            member_mask[:, request_number : request_number + 1], out_down, jnp.zeros_like(out_down)
        )
        output_adapter_delta = output_adapter_delta + jnp.dot(
            input_rows, out_adapters[request_number][1], preferred_element_type=jnp.float32
        )
    partial_out = jnp.dot(
        attended_rows,
        lax.all_gather(output_weight, "seq", axis=1, tiled=True),
        preferred_element_type=jnp.float32,
    )
    summed_output = lax.psum_scatter(
        partial_out.astype(jnp.bfloat16), "sub", scatter_dimension=1, tiled=True
    ).astype(jnp.float32)
    return (summed_output + adapter_scale * output_adapter_delta).astype(jnp.bfloat16)


def solution(mesh):
    return jax.shard_map(
        shards,
        mesh=mesh,
        in_specs=(
            P(("groups", "seq"), None),
            P(),
            P("seq", "sub"),
            P("seq", None, "sub"),
            P("sub", "seq"),
            P("seq", None, None),
            P("seq", None, "sub"),
            P("seq", None, None, "sub"),
            P("seq", "sub", None),
            P("seq", None, "sub"),
            P("groups"),
            P("groups"),
            P(),
        ),
        out_specs=P(("groups", "seq"), "sub"),
        check_vma=False,
    )
```

profile of v0, /device:TPU:0, one launch (start us, length us, event | category | flops | bytes accessed | tf_op | source)
XLA Modules:
  0.0 921.7 jit_solution(15412389674003154354)
XLA Ops:
  27.5 3.2 select_bitcast_fusion.4
  32.4 2.9 select_bitcast_fusion
  39.9 3.2 fusion.10
  43.7 3.6 fusion.12
  47.4 201.5 %all-reduce.3.cloned.1.call-done = (bf16[64,4096]{1,0:T(8,128)(2,1)}, bf16[2048,64]{0,1:T(8,128)(2,1)}, bf16[2,64,512]{2,1,0:T(8,128)(2,1)}, bf16[4096,192]{0,1:...) async-done(((bf16[64,4096]{1,0:T(8,128)(2,1)}, ...) | async-done | bytes 11010064 | tf_op jit(solution)/shard_map/psum | solution.py:16
  248.8 4.4 fusion.28
  260.1 68.9 %all-gather.5.cloned.1.call-done = bf16[4096,2,512]{0,2,1:T(8,128)(2,1)} async-done(((bf16[256,2,512]{0,2,1:T(8,128)(2,1)}), bf16[4096,2,512]{0,2,1:T(8,128)(2,1)}) %all-gather.5.cloned.1.call-update) | async-done | bytes 8388624 | tf_op jit(solution)/shard_map/all_gather | solution.py:81
  328.9 8.2 fusion.14
  340.3 7.0 fusion.9
  347.3 2.7 fusion.36
  350.0 2.7 fusion.38
  352.8 2.7 fusion.42
  358.2 97.6 %all-gather.9.cloned.1.call-done = bf16[4096,2048]{1,0:T(8,128)(2,1)} async-done(((bf16[256,2048]{1,0:T(8,128)(2,1)}), bf16[4096,2048]{1,0:T(8,128)(2,1)}) %all-gather.9.cloned.1.call-update) | async-done | bytes 16777232 | tf_op jit(solution)/shard_map/all_gather | solution.py:80
  455.8 17.9 %add_bitcast_fusion = f32[64,8,16,128]{3,1,2,0:T(8,128)S(1)} fusion(f32[512,2048]{1,0:T(8,128)} %fusion.36, f32[512,2048]{1,0:T(8,128)} %fusion.38, f32[512,2048]{1,0:T(8,128)} %fusion.42, f32[512,2048]{1,0:T(8,128)} %fusion.40, bf16[512,4096]{1,0:T(8,128)(2,1)} %fusion.12, bf16[4096,2048]{1,0:T(8,128)(2,1)} %all-gather.9.cloned.1.call-done), kind=kOutput, calls=%fused_computation.25 | convolution fusion | flops 8595177472 | bytes 41943040 | tf_op jit(solution)/shard_map/dot_general | solution.py:82
  478.6 107.3 %all-gather.7.cloned.1.call-done = bf16[8192,2,512]{0,2,1:T(8,128)(2,1)} async-done(((bf16[512,2,512]{0,2,1:T(8,128)(2,1)}), bf16[8192,2,512]{0,2,1:T(8,128)(2,1)}) %all-gather.7.cloned.1.call-update) | async-done | bytes 16777232 | tf_op jit(solution)/shard_map/all_gather | solution.py:139
  585.9 12.2 %fusion.77 = (bf16[8192,1,512]{0,2,1:T(8,128)(2,1)}, bf16[8192,1,512]{0,2,1:T(8,128)(2,1)}) fusion(bf16[8192,2,512]{0,2,1:T(8,128)(2,1)} %all-gather.7.cloned.1.call-done), kind=kLoop, calls=%fused_computation.150 | loop fusion | bytes 33554432 | tf_op jit(solution)/shard_map/slice | solution.py:143
  598.1 99.5 %fusion = (f32[4,4,512]{2,1,0:T(4,128)S(1)}, f32[4,8192,512,4]{2,1,3,0:T(8,128)}) fusion(pred[512,8192]{0,1:T(8,128)(4,1)} %fusion.9, bf16[8192,4,128,1]{0,2,3,1:T(8,128)(2,1)} %bitcast.164, bf16[512,4,4,64]{3,0,2,1:T(8,128)(2,1)S(1)} %bitcast.166, bf16[512,4,4,64]{3,0,2,1:T(8,128)(2,1)} %bitcast.167), kind=kOutput, calls=%fused_computation.2 | convolution fusion | flops 17385381888 | bytes 283148288 | tf_op jit(solution)/shard_map/xouc,boc->ouxb/dot_general | solution.py:145
  697.6 82.0 %fusion.1 = f32[4,4,512]{2,1,0:T(4,128)S(1)} fusion(f32[4,8192,512,4]{2,1,3,0:T(8,128)} %get-tuple-element.66, f32[4,4,512]{2,1,0:T(4,128)S(1)} %broadcast_maximum_fusion, pred[512,8192]{0,1:T(8,128)(4,1)} %fusion.9), kind=kLoop, calls=%fused_computation.3 | loop fusion | flops 335536128 | bytes 272695296 | tf_op jit(solution)/shard_map/reduce_sum | solution.py:152
  779.6 94.6 %fusion.13 = bf16[512,4,4,128]{0,3,2,1:T(8,128)(2,1)S(1)} fusion(bf16[8192,4,128,1]{0,2,3,1:T(8,128)(2,1)} %bitcast.163, f32[4,8192,512,4]{2,1,3,0:T(8,128)} %get-tuple-element.66, f32[4,4,512]{2,1,0:T(4,128)S(1)} %broadcast_maximum_fusion, pred[512,8192]{0,1:T(8,128)(4,1)} %fusion.9, f32[512,4,4]{0,2,1:T(4,128)S(1)} %bitcast.169), kind=kOutput, calls=%fused_computation.20 | convolution fusion | flops 17517510656 | bytes 283181056 | tf_op jit(solution)/shard_map/kgts,skd->kgtd/dot_general | solution.py:153
  876.4 4.6 fusion.55
  880.9 4.5 fusion.59
  885.4 4.5 fusion.57
  890.0 14.3 %convolution_convert_fusion = bf16[512,4096]{1,0:T(8,128)(2,1)} fusion(bf16[512,2048]{0,1:T(8,128)(2,1)S(1)} %bitcast.162, bf16[2048,4096]{1,0:T(8,128)(2,1)} %all-gather.11.cloned.1.call-done), kind=kOutput, calls=%fused_computation.18 | convolution fusion | flops 8592031744 | bytes 23068672 | tf_op jit(solution)/shard_map/dot_general | solution.py:180
  904.3 10.4 %add_convert_fusion = bf16[512,4096]{1,0:T(8,128)(2,1)} fusion(f32[512,4096]{1,0:T(8,128)} %fusion.55, f32[512,4096]{1,0:T(8,128)S(1)} %copy-done, f32[512,4096]{1,0:T(8,128)} %fusion.57, bf16[512,4096]{1,0:T(8,128)(2,1)} %convolution_convert_fusion, bf16[64,4096]{1,0:T(8,128)(2,1)S(1)} %copy-done.7, bf16[512,64]{0,1:T(8,128)(2,1)S(1)} %fusion.35, ...), kind=kOutput, calls=%fused_computation.17 | convolution fusion | flops 283148288 | bytes 34144768 | tf_op jit(solution)/shard_map/dot_general | solution.py:177
  (130 shorter events, 29.2 us)
Async XLA Ops:
  6.5 25.1 %copy-start.6 = (bf16[2,2,64,512]{3,2,1,0:T(8,128)(2,1)S(1)}, bf16[2,2,64,512]{3,2,1,0:T(8,128)(2,1)}, u32[]{:S(2)}) copy-start(bf16[2,2,64,512]{3,2,1,0:T(8,128)(2,1)} %param.20) | copy-start | bytes 786436
  6.5 25.9 %copy-start.2 = (bf16[2,4096,192]{1,2,0:T(8,128)(2,1)S(1)}, bf16[2,4096,192]{1,2,0:T(8,128)(2,1)}, u32[]{:S(2)}) copy-start(bf16[2,4096,192]{1,2,0:T(8,128)(2,1)} %param.18) | copy-start | bytes 9437188
  6.5 242.3 %all-reduce.3.cloned.1.call-start = ((), (), s32[]{:S(2)}) async-start(), calls=%async_computation.4 | async-start | bytes 22020096 | tf_op jit(solution)/shard_map/psum | solution.py:16
  36.4 292.6 %all-gather.5.cloned.1.call-start = ((), (), s32[]{:S(2)}) async-start(), calls=%async_computation | async-start | bytes 8912896 | tf_op jit(solution)/shard_map/all_gather | solution.py:81
  38.6 417.1 %all-gather.9.cloned.1.call-start = ((), (), s32[]{:S(2)}) async-start(), calls=%async_computation.2 | async-start | bytes 17825792 | tf_op jit(solution)/shard_map/all_gather | solution.py:80
  39.4 546.5 %all-gather.7.cloned.1.call-start = ((), (), s32[]{:S(2)}) async-start(), calls=%async_computation.1 | async-start | bytes 17825792 | tf_op jit(solution)/shard_map/all_gather | solution.py:139
  39.8 209.0 %copy-start.26 = (pred[512]{0:T(512)(128)(4,1)}, pred[512]{0:T(512)(128)(4,1)S(1)}, u32[]{:S(2)}) copy-start(pred[512]{0:T(512)(128)(4,1)S(1)} %get-tuple-element.8) | copy-start | bytes 1540
  39.8 214.1 %copy-start.24 = (pred[512]{0:T(512)(128)(4,1)}, pred[512]{0:T(512)(128)(4,1)S(1)}, u32[]{:S(2)}) copy-start(pred[512]{0:T(512)(128)(4,1)S(1)} %get-tuple-element.7) | copy-start | bytes 1540
  39.8 216.4 %copy-start.28 = (pred[512]{0:T(512)(128)(4,1)}, pred[512]{0:T(512)(128)(4,1)S(1)}, u32[]{:S(2)}) copy-start(pred[512]{0:T(512)(128)(4,1)S(1)} %get-tuple-element.6) | copy-start | bytes 1540
  39.8 218.7 %copy-start.31 = (pred[512]{0:T(512)(128)(4,1)}, pred[512]{0:T(512)(128)(4,1)S(1)}, u32[]{:S(2)}) copy-start(pred[512]{0:T(512)(128)(4,1)S(1)} %get-tuple-element.5) | copy-start | bytes 1540
  248.8 5.1 copy-start.3
  248.8 5.1 copy-start.35
  260.0 77.1 %copy-start.20 = (bf16[2,64,512]{2,1,0:T(8,128)(2,1)S(1)}, bf16[2,64,512]{2,1,0:T(8,128)(2,1)}, u32[]{:S(2)}) copy-start(bf16[2,64,512]{2,1,0:T(8,128)(2,1)} %get-tuple-element.17) | copy-start | bytes 393220
  338.2 9.1 copy-start.15
  339.3 550.7 %all-gather.11.cloned.1.call-start = ((), (), s32[]{:S(2)}) async-start(), calls=%async_computation.3 | async-start | bytes 17825792 | tf_op jit(solution)/shard_map/all_gather | solution.py:182
  340.3 9.7 %copy-start.14 = (bf16[64,2048]{1,0:T(8,128)(2,1)S(1)}, bf16[64,2048]{1,0:T(8,128)(2,1)}, u32[]{:S(2)}) copy-start(bf16[64,2048]{1,0:T(8,128)(2,1)} %get-tuple-element.20) | copy-start | bytes 786436
  347.3 5.4 copy-start.13
  350.0 5.5 copy-start.12
  779.6 94.7 %copy-start.19 = (bf16[2048,64]{0,1:T(8,128)(2,1)S(1)}, bf16[2048,64]{0,1:T(8,128)(2,1)}, u32[]{:S(2)}) copy-start(bf16[2048,64]{0,1:T(8,128)(2,1)} %get-tuple-element.10) | copy-start | bytes 786436
  779.6 94.7 %copy-start.27 = (pred[512]{0:T(512)(128)(4,1)S(1)}, pred[512]{0:T(512)(128)(4,1)}, u32[]{:S(2)}) copy-start(pred[512]{0:T(512)(128)(4,1)} %copy-done.26) | copy-start | bytes 1540
  779.6 95.2 %copy-start.18 = (bf16[2048,64]{0,1:T(8,128)(2,1)S(1)}, bf16[2048,64]{0,1:T(8,128)(2,1)}, u32[]{:S(2)}) copy-start(bf16[2048,64]{0,1:T(8,128)(2,1)} %get-tuple-element.23) | copy-start | bytes 786436
  779.6 95.2 %copy-start.25 = (pred[512]{0:T(512)(128)(4,1)S(1)}, pred[512]{0:T(512)(128)(4,1)}, u32[]{:S(2)}) copy-start(pred[512]{0:T(512)(128)(4,1)} %copy-done.24) | copy-start | bytes 1540
  890.0 14.3 %copy-start.7 = (bf16[64,4096]{1,0:T(8,128)(2,1)S(1)}, bf16[64,4096]{1,0:T(8,128)(2,1)}, u32[]{:S(2)}) copy-start(bf16[64,4096]{1,0:T(8,128)(2,1)} %get-tuple-element.28) | copy-start | bytes 1572868
  890.0 14.3 %copy-start = (f32[512,4096]{1,0:T(8,128)S(1)}, f32[512,4096]{1,0:T(8,128)}, u32[]{:S(2)}) copy-start(f32[512,4096]{1,0:T(8,128)} %fusion.59) | copy-start | bytes 25165828
  (18 other events, 46.0 us)
Sparse Core Ops, SparseCore 0:
  36.5 212.3 all-reduce.2
  251.0 77.9 all-gather.4
  331.1 124.5 all-gather.8
  457.8 128.0 all-gather.6
  587.9 128.0 all-gather.10
where the time goes:
time: 932 us; the launch traced here: 922 us
  waiting for transfers between devices  476 us (51%)
  matrix products  283 us (30%)
  other arithmetic  109 us (12%)
  between operations  32.2 us (3%)
  local copies, waits for them, and re-layouts  21.2 us (2%)
    psum x1, waiting for transfers between devices, spread(): return lax.psum(jnp.where(mine, shard, jnp.zeros_like(shard)), axis)  201 us
    all_gather x1, waiting for transfers between devices, shards(): piece = lax.all_gather(kv_rows, 'seq', axis=0, tiled=True)  107 us
    dot_general x1, matrix products, shards(): jnp.einsum('xouc,boc->ouxb', queries, key_heads, preferred_element_type=j...  99.5 us
    all_gather x1, waiting for transfers between devices, shards(): piece_query = lax.all_gather(query_weight, 'seq', axis=0, tiled=True)  97.6 us
    dot_general x1, matrix products, shards(): jnp.einsum('kgts,skd->kgtd', weights.astype(jnp.bfloat16), value_heads, p...  94.6 us
    reduce_sum x1, other arithmetic, shards(): running_sum = jnp.sum(weights, axis=-1)  82 us
    all_gather x1, waiting for transfers between devices, shards(): piece_kv = lax.all_gather(key_value_weight, 'seq', axis=0, tiled=True)  68.9 us
    dot_general x4, matrix products, shards(): jnp.dot(input_rows, out_adapters[request_number][1], preferred_element_ty...  24 us
  transfers between devices with their start and end apart: 5, of which 4 were waited for; matrix products, arithmetic and copies ran while one was open for 41% of the time, Pallas kernels for 0%

commit v1 on v0

--- a/solution.py
+++ b/solution.py
@@ -9,6 +9,27 @@
 adapter_scale = 2.0
 rope_base = 10000.0
 neg_big = -1e30
+
+
+def collect(x, axis, dim):
+    size, index, rows = (lax.axis_size(axis), lax.axis_index(axis), x.shape[dim])
+    right = [(i, (i + 1) % size) for i in range(size)]
+    left = [(i, (i - 1) % size) for i in range(size)]
+    filled = jnp.zeros((*x.shape[:dim], size * rows, *x.shape[dim + 1 :]), x.dtype)
+    filled = lax.dynamic_update_slice_in_dim(filled, x, index * rows, axis=dim)
+    from_left = from_right = x
+    middle = size // 2
+    for lap in range(1, middle + 1):
+        from_left = lax.ppermute(from_left, axis, right)
+        filled = lax.dynamic_update_slice_in_dim(
+            filled, from_left, (index - lap) % size * rows, axis=dim
+        )
+        if lap < size - middle:
+            from_right = lax.ppermute(from_right, axis, left)
+            filled = lax.dynamic_update_slice_in_dim(
+                filled, from_right, (index + lap) % size * rows, axis=dim
+            )
+    return filled
 
 
 def spread(shard, axis, root):
@@ -136,7 +157,7 @@
         jnp.bfloat16
     )
     kv_rows = jnp.stack([key_row_list.reshape(row_total, kv_cols), value_row_list], axis=1)
-    piece = lax.all_gather(kv_rows, "seq", axis=0, tiled=True)
+    piece = collect(kv_rows, "seq", 0)
     running_max = jnp.full((key_value_heads, group_width, row_total), neg_big, jnp.float32)
     piece_len = piece.shape[0]
     key_pos = jnp.arange(piece_len, dtype=jnp.int32)

time: 932 us -> 974 us (1.045)
  starting transfers between devices: 0.34 us -> 68.3 us
  waiting for transfers between devices: 476 us -> 418 us
  local copies, waits for them, and re-layouts: 21.2 us -> 53.2 us
    ppermute x0 -> x15, waiting for transfers between devices: none -> 147 us  [the longest x8 137 us: collect(): from_left = lax.ppermute(from_left, axis, right)]
    all_gather x1 -> x0, waiting for transfers between devices: 107 us -> none  [shards(): piece = lax.all_gather(kv_rows, 'seq', axis=0, tiled=True)]
    all_gather x1, waiting for transfers between devices: 97.6 us -> 0.01 us  [shards(): piece_query = lax.all_gather(query_weight, 'seq', axis=0, tiled=True)]
    ppermute x0 -> x15, starting transfers between devices: none -> 68.2 us  [the longest x8 47.6 us: collect(): from_left = lax.ppermute(from_left, axis, right)]
    dynamic_update_slice x0 -> x15, local copies, waits for them, and re-layouts: none -> 22.5 us  [the longest x7 11.5 us: collect(): lax.dynamic_update_slice_in_dim(filled, from_right, (index + lap) % size...]
  transfers between devices with their start and end apart: 5 -> 19, of which waited for: 4 -> 11; matrix products, arithmetic and copies ran while one was open for 41% -> 42% of each run, Pallas kernels for 0% -> 0%
where the time goes in v1:
time: 974 us; the launch traced here: 966 us
  waiting for transfers between devices  418 us (43%)
  matrix products  285 us (29%)
  other arithmetic  109 us (11%)
  starting transfers between devices  68.3 us (7%)
  local copies, waits for them, and re-layouts  53.2 us (5%)
  between operations  32.3 us (3%)
    psum x1, waiting for transfers between devices, spread(): return lax.psum(jnp.where(mine, shard, jnp.zeros_like(shard)), axis)  201 us
    ppermute x8, waiting for transfers between devices, collect(): from_left = lax.ppermute(from_left, axis, right)  137 us
    dot_general x1, matrix products, shards(): jnp.einsum('xouc,boc->ouxb', queries, key_heads, preferred_element_type=j...  97.5 us
    dot_general x1, matrix products, shards(): jnp.einsum('kgts,skd->kgtd', weights.astype(jnp.bfloat16), value_heads, p...  94.6 us
    reduce_sum x1, other arithmetic, shards(): running_sum = jnp.sum(weights, axis=-1)  82 us
    all_gather x1, waiting for transfers between devices, shards(): piece_kv = lax.all_gather(key_value_weight, 'seq', axis=0, tiled=True)  68.8 us
    ppermute x8, starting transfers between devices, collect(): from_left = lax.ppermute(from_left, axis, right)  47.6 us
    dot_general x4, matrix products, shards(): jnp.dot(input_rows, out_adapters[request_number][1], preferred_element_ty...  24.1 us
  transfers between devices with their start and end apart: 19, of which 11 were waited for; matrix products, arithmetic and copies ran while one was open for 42% of the time, Pallas kernels for 0%

profile of v1, /device:TPU:0, one launch (start us, length us, event | category | flops | bytes accessed | tf_op | source)
XLA Modules:
  0.0 965.7 jit_solution(14827432678623315927)
XLA Ops:
  47.4 201.4 %all-reduce.3.cloned.1.call-done = (bf16[64,4096]{1,0:T(8,128)(2,1)}, bf16[2048,64]{0,1:T(8,128)(2,1)}, bf16[2,64,512]{2,1,0:T(8,128)(2,1)}, bf16[4096,192]{0,1:...) async-done(((bf16[64,4096]{1,0:T(8,128)(2,1)}, ...) | async-done | bytes 11010064 | tf_op jit(solution)/shard_map/psum | solution.py:37
  260.1 68.8 %all-gather.4.cloned.1.call-done = bf16[4096,2,512]{0,2,1:T(8,128)(2,1)} async-done(((bf16[256,2,512]{0,2,1:T(8,128)(2,1)}), bf16[4096,2,512]{0,2,1:T(8,128)(2,1)}) %all-gather.4.cloned.1.call-update) | async-done | bytes 8388624 | tf_op jit(solution)/shard_map/all_gather | solution.py:102
  328.9 8.7 fusion.14
  338.7 6.0 broadcast_in_dim.138
  350.3 35.1 %collective-permute-done = bf16[512,2,512]{0,2,1:T(8,128)(2,1)S(1)} collective-permute-done((bf16[512,2,512]{0,2,1:T(8,128)(2,1)S(1)}, bf16[512,2,512]{0,2,1:T(8,128)(2,1)S(1)}, u32[]{:S(2)}, u32[]{:S(2)}) %collective-permute-start) | collective-permute-done | bytes 1048608 | tf_op jit(solution)/shard_map/ppermute | solution.py:23
  389.9 24.4 %collective-permute-done.2 = bf16[512,2,512]{0,2,1:T(8,128)(2,1)S(1)} collective-permute-done((bf16[512,2,512]{0,2,1:T(8,128)(2,1)S(1)}, bf16[512,2,512]{0,2,1:T(8,128)(2,1)S(1)}, u32[]{:S(2)}, u32[]{:S(2)}) %collective-permute-start.2) | collective-permute-done | bytes 1048608 | tf_op jit(solution)/shard_map/ppermute | solution.py:23
  414.3 9.3 collective-permute-done.3
  428.3 24.9 %collective-permute-done.4 = bf16[512,2,512]{0,2,1:T(8,128)(2,1)S(1)} collective-permute-done((bf16[512,2,512]{0,2,1:T(8,128)(2,1)S(1)}, bf16[512,2,512]{0,2,1:T(8,128)(2,1)S(1)}, u32[]{:S(2)}, u32[]{:S(2)}) %collective-permute-start.4) | collective-permute-done | bytes 1048608 | tf_op jit(solution)/shard_map/ppermute | solution.py:23
  457.6 12.6 %collective-permute-done.6 = bf16[512,2,512]{0,2,1:T(8,128)(2,1)S(1)} collective-permute-done((bf16[512,2,512]{0,2,1:T(8,128)(2,1)S(1)}, bf16[512,2,512]{0,2,1:T(8,128)(2,1)S(1)}, u32[]{:S(2)}, u32[]{:S(2)}) %collective-permute-start.6) | collective-permute-done | bytes 1048608 | tf_op jit(solution)/shard_map/ppermute | solution.py:23
  470.3 19.5 %collective-permute-start.8 = (bf16[512,2,512]{0,2,1:T(8,128)(2,1)S(1)}, bf16[512,2,512]{0,2,1:T(8,128)(2,1)}, u32[]{:S(2)}, u32[]{:S(2)}) collective-permute-start(bf16[512,2,512]{0,2,1:T(8,128)(2,1)S(1)} %collective-permute-done.6), channel_id=1, source_target_pairs={{0,1},{1,2},{2,3},{3,4},{4,5},{5,6},{6,7},{7,8},{8,9},{9,10},{10,1... | collective-permute-start | bytes 3145736 | tf_op jit(solution)/shard_map/ppermute | solution.py:23
  490.0 7.5 collective-permute-done.8
  497.6 12.0 %collective-permute-start.10 = (bf16[512,2,512]{0,2,1:T(8,128)(2,1)}, bf16[512,2,512]{0,2,1:T(8,128)(2,1)}, u32[]{:S(2)}, u32[]{:S(2)}) collective-permute-start(bf16[512,2,512]{0,2,1:T(8,128)(2,1)} %collective-permute-done.8), channel_id=1, source_target_pairs={{0,1},{1,2},{2,3},{3,4},{4,5},{5,6},{6,7},{7,8},{8,9},{9,10},{10,1... | collective-permute-start | bytes 3145736 | tf_op jit(solution)/shard_map/ppermute | solution.py:23
  509.6 6.9 fusion.9
  530.8 5.3 collective-permute-start.12
  550.5 12.5 %collective-permute-done.12 = bf16[512,2,512]{0,2,1:T(8,128)(2,1)S(1)} collective-permute-done((bf16[512,2,512]{0,2,1:T(8,128)(2,1)}, bf16[512,2,512]{0,2,1:T(8,128)(2,1)S(1)}, u32[]{:S(2)}, u32[]{:S(2)}) %collective-permute-start.12) | collective-permute-done | bytes 1048608 | tf_op jit(solution)/shard_map/ppermute | solution.py:23
  563.1 10.5 %collective-permute-start.14 = (bf16[512,2,512]{0,2,1:T(8,128)(2,1)S(1)}, bf16[512,2,512]{0,2,1:T(8,128)(2,1)S(1)}, u32[]{:S(2)}, u32[]{:S(2)}) collective-permute-start(bf16[512,2,512]{0,2,1:T(8,128)(2,1)S(1)} %collective-permute-done.12), channel_id=1, source_target_pairs={{0,1},{1,2},{2,3},{3,4},{4,5},{5,6},{6,7},{7,8},{8,9},{9,10},{10,1... | collective-permute-start | bytes 3145736 | tf_op jit(solution)/shard_map/ppermute | solution.py:23
  587.0 18.7 %collective-permute-done.14 = bf16[512,2,512]{0,2,1:T(8,128)(2,1)S(1)} collective-permute-done((bf16[512,2,512]{0,2,1:T(8,128)(2,1)S(1)}, bf16[512,2,512]{0,2,1:T(8,128)(2,1)S(1)}, u32[]{:S(2)}, u32[]{:S(2)}) %collective-permute-start.14) | collective-permute-done | bytes 1048608 | tf_op jit(solution)/shard_map/ppermute | solution.py:23
  606.8 14.3 %fusion.77 = (bf16[8192,1,512]{0,2,1:T(8,128)(2,1)}, bf16[8192,1,512]{0,2,1:T(8,128)(2,1)}) fusion(bf16[8192,2,512]{0,2,1:T(8,128)(2,1)} %constant_dynamic-update-slice_fusion), kind=kLoop, calls=%fused_computation.166 | loop fusion | bytes 33554432 | tf_op jit(solution)/shard_map/slice | solution.py:164
  621.1 17.9 %add_bitcast_fusion = f32[64,8,16,128]{3,1,2,0:T(8,128)S(1)} fusion(f32[512,2048]{1,0:T(8,128)} %fusion.36, f32[512,2048]{1,0:T(8,128)} %fusion.38, f32[512,2048]{1,0:T(8,128)} %fusion.42, f32[512,2048]{1,0:T(8,128)} %fusion.40, bf16[512,4096]{1,0:T(8,128)(2,1)} %fusion.12, bf16[4096,2048]{1,0:T(8,128)(2,1)} %all-gather.6.cloned.1.call-done), kind=kOutput, calls=%fused_computation.25 | convolution fusion | flops 8595177472 | bytes 41943040 | tf_op jit(solution)/shard_map/dot_general | solution.py:103
  644.0 97.5 %fusion = (f32[4,4,512]{2,1,0:T(4,128)S(1)}, f32[4,8192,512,4]{2,1,3,0:T(8,128)}) fusion(pred[512,8192]{0,1:T(8,128)(4,1)} %fusion.9, bf16[8192,4,128,1]{0,2,3,1:T(8,128)(2,1)} %bitcast.164, bf16[512,4,4,64]{3,0,2,1:T(8,128)(2,1)S(1)} %bitcast.166, bf16[512,4,4,64]{3,0,2,1:T(8,128)(2,1)} %bitcast.167), kind=kOutput, calls=%fused_computation.2 | convolution fusion | flops 17385381888 | bytes 283148288 | tf_op jit(solution)/shard_map/xouc,boc->ouxb/dot_general | solution.py:166
  741.5 82.0 %fusion.1 = f32[4,4,512]{2,1,0:T(4,128)S(1)} fusion(f32[4,8192,512,4]{2,1,3,0:T(8,128)} %get-tuple-element.68, f32[4,4,512]{2,1,0:T(4,128)S(1)} %broadcast_maximum_fusion, pred[512,8192]{0,1:T(8,128)(4,1)} %fusion.9), kind=kLoop, calls=%fused_computation.3 | loop fusion | flops 335536128 | bytes 272695296 | tf_op jit(solution)/shard_map/reduce_sum | solution.py:173
  823.5 94.6 %fusion.13 = bf16[512,4,4,128]{0,3,2,1:T(8,128)(2,1)S(1)} fusion(bf16[8192,4,128,1]{0,2,3,1:T(8,128)(2,1)} %bitcast.163, f32[4,8192,512,4]{2,1,3,0:T(8,128)} %get-tuple-element.68, f32[4,4,512]{2,1,0:T(4,128)S(1)} %broadcast_maximum_fusion, pred[512,8192]{0,1:T(8,128)(4,1)} %fusion.9, f32[512,4,4]{0,2,1:T(4,128)S(1)} %bitcast.169), kind=kOutput, calls=%fused_computation.20 | convolution fusion | flops 17517510656 | bytes 283181056 | tf_op jit(solution)/shard_map/kgts,skd->kgtd/dot_general | solution.py:174
  934.0 14.3 %convolution_convert_fusion = bf16[512,4096]{1,0:T(8,128)(2,1)} fusion(bf16[512,2048]{0,1:T(8,128)(2,1)S(1)} %bitcast.162, bf16[2048,4096]{1,0:T(8,128)(2,1)} %all-gather.8.cloned.1.call-done), kind=kOutput, calls=%fused_computation.18 | convolution fusion | flops 8592031744 | bytes 23068672 | tf_op jit(solution)/shard_map/dot_general | solution.py:201
  948.3 10.3 %add_convert_fusion = bf16[512,4096]{1,0:T(8,128)(2,1)} fusion(f32[512,4096]{1,0:T(8,128)} %fusion.55, f32[512,4096]{1,0:T(8,128)S(1)} %copy-done, f32[512,4096]{1,0:T(8,128)} %fusion.57, bf16[512,4096]{1,0:T(8,128)(2,1)} %convolution_convert_fusion, bf16[64,4096]{1,0:T(8,128)(2,1)S(1)} %copy-done.15, bf16[512,64]{0,1:T(8,128)(2,1)S(1)} %fusion.35, ...), kind=kOutput, calls=%fused_computation.17 | convolution fusion | flops 283148288 | bytes 34144768 | tf_op jit(solution)/shard_map/dot_general | solution.py:198
  (195 shorter events, 118.1 us)
Async XLA Ops:
  6.5 242.3 %all-reduce.3.cloned.1.call-start = ((), (), s32[]{:S(2)}) async-start(), calls=%async_computation.3 | async-start | bytes 22020096 | tf_op jit(solution)/shard_map/psum | solution.py:37
  36.4 292.5 %all-gather.4.cloned.1.call-start = ((), (), s32[]{:S(2)}) async-start(), calls=%async_computation | async-start | bytes 8912896 | tf_op jit(solution)/shard_map/all_gather | solution.py:102
  38.6 582.5 %all-gather.6.cloned.1.call-start = ((), (), s32[]{:S(2)}) async-start(), calls=%async_computation.1 | async-start | bytes 17825792 | tf_op jit(solution)/shard_map/all_gather | solution.py:101
  39.4 894.6 %all-gather.8.cloned.1.call-start = ((), (), s32[]{:S(2)}) async-start(), calls=%async_computation.2 | async-start | bytes 17825792 | tf_op jit(solution)/shard_map/all_gather | solution.py:203
  39.8 209.0 %copy-start.37 = (pred[512]{0:T(512)(128)(4,1)}, pred[512]{0:T(512)(128)(4,1)S(1)}, u32[]{:S(2)}) copy-start(pred[512]{0:T(512)(128)(4,1)S(1)} %get-tuple-element.8) | copy-start | bytes 1540
  39.8 214.1 %copy-start.35 = (pred[512]{0:T(512)(128)(4,1)}, pred[512]{0:T(512)(128)(4,1)S(1)}, u32[]{:S(2)}) copy-start(pred[512]{0:T(512)(128)(4,1)S(1)} %get-tuple-element.7) | copy-start | bytes 1540
  39.8 216.4 %copy-start.39 = (pred[512]{0:T(512)(128)(4,1)}, pred[512]{0:T(512)(128)(4,1)S(1)}, u32[]{:S(2)}) copy-start(pred[512]{0:T(512)(128)(4,1)S(1)} %get-tuple-element.6) | copy-start | bytes 1540
  39.8 218.7 %copy-start.42 = (pred[512]{0:T(512)(128)(4,1)}, pred[512]{0:T(512)(128)(4,1)S(1)}, u32[]{:S(2)}) copy-start(pred[512]{0:T(512)(128)(4,1)S(1)} %get-tuple-element.5) | copy-start | bytes 1540
  345.9 39.5 %collective-permute-start = (bf16[512,2,512]{0,2,1:T(8,128)(2,1)S(1)}, bf16[512,2,512]{0,2,1:T(8,128)(2,1)S(1)}, u32[]{:S(2)}, u32[]{:S(2)}) collective-permute-start(bf16[512,2,512]{0,2,1:T(8,128)(2,1)S(1)} %get-tuple-element.39), channel_id=1, source_target_pairs={{0,1},{1,2},{2,3},{3,4},{4,5},{5,6},{6,7},{7,8},{8,9},{9,10},{10,1... | collective-permute-start | bytes 3145736 | tf_op jit(solution)/shard_map/ppermute | solution.py:23
  346.2 39.3 %collective-permute-start.1 = (bf16[512,2,512]{0,2,1:T(8,128)(2,1)S(1)}, bf16[512,2,512]{0,2,1:T(8,128)(2,1)S(1)}, u32[]{:S(2)}, u32[]{:S(2)}) collective-permute-start(bf16[512,2,512]{0,2,1:T(8,128)(2,1)S(1)} %get-tuple-element.39), channel_id=1, source_target_pairs={{0,15},{1,0},{2,1},{3,2},{4,3},{5,4},{6,5},{7,6},{8,7},{9,8},{10,9... | collective-permute-start | bytes 3145736 | tf_op jit(solution)/shard_map/ppermute | solution.py:28
  385.4 28.9 %collective-permute-start.2 = (bf16[512,2,512]{0,2,1:T(8,128)(2,1)S(1)}, bf16[512,2,512]{0,2,1:T(8,128)(2,1)S(1)}, u32[]{:S(2)}, u32[]{:S(2)}) collective-permute-start(bf16[512,2,512]{0,2,1:T(8,128)(2,1)S(1)} %collective-permute-done), channel_id=1, source_target_pairs={{0,1},{1,2},{2,3},{3,4},{4,5},{5,6},{6,7},{7,8},{8,9},{9,10},{10,1... | collective-permute-start | bytes 3145736 | tf_op jit(solution)/shard_map/ppermute | solution.py:23
  385.4 38.2 %collective-permute-start.3 = (bf16[512,2,512]{0,2,1:T(8,128)(2,1)S(1)}, bf16[512,2,512]{0,2,1:T(8,128)(2,1)S(1)}, u32[]{:S(2)}, u32[]{:S(2)}) collective-permute-start(bf16[512,2,512]{0,2,1:T(8,128)(2,1)S(1)} %collective-permute-done.1), channel_id=1, source_target_pairs={{0,15},{1,0},{2,1},{3,2},{4,3},{5,4},{6,5},{7,6},{8,7},{9,8},{10,9... | collective-permute-start | bytes 3145736 | tf_op jit(solution)/shard_map/ppermute | solution.py:28
  414.3 38.9 %collective-permute-start.4 = (bf16[512,2,512]{0,2,1:T(8,128)(2,1)S(1)}, bf16[512,2,512]{0,2,1:T(8,128)(2,1)S(1)}, u32[]{:S(2)}, u32[]{:S(2)}) collective-permute-start(bf16[512,2,512]{0,2,1:T(8,128)(2,1)S(1)} %collective-permute-done.2), channel_id=1, source_target_pairs={{0,1},{1,2},{2,3},{3,4},{4,5},{5,6},{6,7},{7,8},{8,9},{9,10},{10,1... | collective-permute-start | bytes 3145736 | tf_op jit(solution)/shard_map/ppermute | solution.py:23
  423.7 29.5 %collective-permute-start.5 = (bf16[512,2,512]{0,2,1:T(8,128)(2,1)S(1)}, bf16[512,2,512]{0,2,1:T(8,128)(2,1)}, u32[]{:S(2)}, u32[]{:S(2)}) collective-permute-start(bf16[512,2,512]{0,2,1:T(8,128)(2,1)S(1)} %collective-permute-done.3), channel_id=1, source_target_pairs={{0,15},{1,0},{2,1},{3,2},{4,3},{5,4},{6,5},{7,6},{8,7},{9,8},{10,9... | collective-permute-start | bytes 3145736 | tf_op jit(solution)/shard_map/ppermute | solution.py:28
  453.2 17.1 %collective-permute-start.6 = (bf16[512,2,512]{0,2,1:T(8,128)(2,1)S(1)}, bf16[512,2,512]{0,2,1:T(8,128)(2,1)S(1)}, u32[]{:S(2)}, u32[]{:S(2)}) collective-permute-start(bf16[512,2,512]{0,2,1:T(8,128)(2,1)S(1)} %collective-permute-done.4), channel_id=1, source_target_pairs={{0,1},{1,2},{2,3},{3,4},{4,5},{5,6},{6,7},{7,8},{8,9},{9,10},{10,1... | collective-permute-start | bytes 3145736 | tf_op jit(solution)/shard_map/ppermute | solution.py:23
  453.2 36.8 %collective-permute-start.7 = (bf16[512,2,512]{0,2,1:T(8,128)(2,1)}, bf16[512,2,512]{0,2,1:T(8,128)(2,1)}, u32[]{:S(2)}, u32[]{:S(2)}) collective-permute-start(bf16[512,2,512]{0,2,1:T(8,128)(2,1)} %collective-permute-done.5), channel_id=1, source_target_pairs={{0,15},{1,0},{2,1},{3,2},{4,3},{5,4},{6,5},{7,6},{8,7},{9,8},{10,9... | collective-permute-start | bytes 3145736 | tf_op jit(solution)/shard_map/ppermute | solution.py:28
  470.3 27.3 %collective-permute-start.8 = (bf16[512,2,512]{0,2,1:T(8,128)(2,1)S(1)}, bf16[512,2,512]{0,2,1:T(8,128)(2,1)}, u32[]{:S(2)}, u32[]{:S(2)}) collective-permute-start(bf16[512,2,512]{0,2,1:T(8,128)(2,1)S(1)} %collective-permute-done.6), channel_id=1, source_target_pairs={{0,1},{1,2},{2,3},{3,4},{4,5},{5,6},{6,7},{7,8},{8,9},{9,10},{10,1... | collective-permute-start | bytes 3145736 | tf_op jit(solution)/shard_map/ppermute | solution.py:23
  490.0 35.7 %collective-permute-start.9 = (bf16[512,2,512]{0,2,1:T(8,128)(2,1)}, bf16[512,2,512]{0,2,1:T(8,128)(2,1)}, u32[]{:S(2)}, u32[]{:S(2)}) collective-permute-start(bf16[512,2,512]{0,2,1:T(8,128)(2,1)} %collective-permute-done.7), channel_id=1, source_target_pairs={{0,15},{1,0},{2,1},{3,2},{4,3},{5,4},{6,5},{7,6},{8,7},{9,8},{10,9... | collective-permute-start | bytes 3145736 | tf_op jit(solution)/shard_map/ppermute | solution.py:28
  497.6 33.2 %collective-permute-start.10 = (bf16[512,2,512]{0,2,1:T(8,128)(2,1)}, bf16[512,2,512]{0,2,1:T(8,128)(2,1)}, u32[]{:S(2)}, u32[]{:S(2)}) collective-permute-start(bf16[512,2,512]{0,2,1:T(8,128)(2,1)} %collective-permute-done.8), channel_id=1, source_target_pairs={{0,1},{1,2},{2,3},{3,4},{4,5},{5,6},{6,7},{7,8},{8,9},{9,10},{10,1... | collective-permute-start | bytes 3145736 | tf_op jit(solution)/shard_map/ppermute | solution.py:23
  525.7 19.5 %collective-permute-start.11 = (bf16[512,2,512]{0,2,1:T(8,128)(2,1)}, bf16[512,2,512]{0,2,1:T(8,128)(2,1)S(1)}, u32[]{:S(2)}, u32[]{:S(2)}) collective-permute-start(bf16[512,2,512]{0,2,1:T(8,128)(2,1)} %collective-permute-done.9), channel_id=1, source_target_pairs={{0,15},{1,0},{2,1},{3,2},{4,3},{5,4},{6,5},{7,6},{8,7},{9,8},{10,9... | collective-permute-start | bytes 3145736 | tf_op jit(solution)/shard_map/ppermute | solution.py:28
  530.8 32.3 %collective-permute-start.12 = (bf16[512,2,512]{0,2,1:T(8,128)(2,1)}, bf16[512,2,512]{0,2,1:T(8,128)(2,1)S(1)}, u32[]{:S(2)}, u32[]{:S(2)}) collective-permute-start(bf16[512,2,512]{0,2,1:T(8,128)(2,1)} %collective-permute-done.10), channel_id=1, source_target_pairs={{0,1},{1,2},{2,3},{3,4},{4,5},{5,6},{6,7},{7,8},{8,9},{9,10},{10,1... | collective-permute-start | bytes 3145736 | tf_op jit(solution)/shard_map/ppermute | solution.py:23
  545.2 40.7 %collective-permute-start.13 = (bf16[512,2,512]{0,2,1:T(8,128)(2,1)S(1)}, bf16[512,2,512]{0,2,1:T(8,128)(2,1)S(1)}, u32[]{:S(2)}, u32[]{:S(2)}) collective-permute-start(bf16[512,2,512]{0,2,1:T(8,128)(2,1)S(1)} %collective-permute-done.11), channel_id=1, source_target_pairs={{0,15},{1,0},{2,1},{3,2},{4,3},{5,4},{6,5},{7,6},{8,7},{9,8},{10,9... | collective-permute-start | bytes 3145736 | tf_op jit(solution)/shard_map/ppermute | solution.py:28
  563.1 42.6 %collective-permute-start.14 = (bf16[512,2,512]{0,2,1:T(8,128)(2,1)S(1)}, bf16[512,2,512]{0,2,1:T(8,128)(2,1)S(1)}, u32[]{:S(2)}, u32[]{:S(2)}) collective-permute-start(bf16[512,2,512]{0,2,1:T(8,128)(2,1)S(1)} %collective-permute-done.12), channel_id=1, source_target_pairs={{0,1},{1,2},{2,3},{3,4},{4,5},{5,6},{6,7},{7,8},{8,9},{9,10},{10,1... | collective-permute-start | bytes 3145736 | tf_op jit(solution)/shard_map/ppermute | solution.py:23
  823.5 95.2 %copy-start.25 = (bf16[2048,64]{0,1:T(8,128)(2,1)S(1)}, bf16[2048,64]{0,1:T(8,128)(2,1)}, u32[]{:S(2)}) copy-start(bf16[2048,64]{0,1:T(8,128)(2,1)} %get-tuple-element.23) | copy-start | bytes 786436
  (43 other events, 742.3 us)
Sparse Core Ops, SparseCore 0:
  36.5 212.2 all-reduce.2
  250.9 77.9 all-gather.3
  331.1 194.3 all-gather.5
  527.5 159.3 all-gather.7
